TPU v7x, 256 devices: a whole 4x4x8 slice. The times are simulated.
256 devices in a mesh: rows: 64 (over z, y, core), cols: 4 (over x).
Axes of the slice: x: 4, y: 4, z: 8, core: 2. Of those that a mesh axis runs over, the one named last changes fastest.
Arguments:
- feats_t: bfloat16 [128, 131072], P('cols', 'rows'), may hold values from -6 to 6
- adj_index: int32 [1024, 16], replicated, may hold values from 0 to 1023, as said below
- adj_weight: bfloat16 [1024, 16, 128, 128], P('rows'), as said below
- weight: bfloat16 [128, 256], replicated, may hold values from -0.5 to 0.5
- cotangent_t: bfloat16 [256, 131072], P('cols', 'rows'), may hold values from -6 to 6
Outputs:
- output_t: bfloat16 [256, 131072], P('cols', 'rows')
- weight_grad: float32 [128, 256], P('cols')
- feat_grad: float32 [128, 131072], P('cols', 'rows')
Inputs may be any that keep to these rules, and one draw needn't show every extreme that they name: `adj_index`: slot 0 of row block i names block i itself. Blocks are grouped 16 to a device in order. Slot 1 names a block of the next device (device index plus one, cyclically). The row blocks of one device name at most 4 distinct blocks of any other device, and exactly 4 of the next one. A block may stand in several slots of one row block. `adj_weight`: Nonnegative; about one entry in eight is nonzero.
All inputs are finite; a program needn't handle non-finite values.
Results may differ from a plain program's by a relative error of at most 0.0054.
Values may be sent and summed in bfloat16 or wider, within the bound.
A program may use at most 128 MiB of HBM per device.

v0:
```python
import math
import jax
import jax.numpy as jnp
from jax import lax
from jax.sharding import PartitionSpec as P


def body(feats_t, adj_index, adj_weight, weight, cotangent_t):
    feat_rows, node_cols = feats_t.shape
    blocks_n = adj_weight.shape[0]
    slots_n = adj_weight.shape[1]
    tile_n = adj_weight.shape[2]
    row_devs = lax.axis_size("rows")
    row_pos = lax.axis_index("rows")
    col_pos = lax.axis_index("cols")
    unit_rows = cotangent_t.shape[0]
    own_index = lax.dynamic_slice_in_dim(adj_index, row_pos * blocks_n, blocks_n, 0)
    own_flat = own_index.reshape(-1)
    local_tiles = feats_t.reshape(feat_rows, blocks_n, tile_n).transpose(1, 0, 2)
    whole_panel = lax.all_gather(local_tiles, "rows", axis=0, tiled=True)
    picked = whole_panel[own_index]
    aggregate = jnp.einsum("bkfj,bkij->fbi", picked, adj_weight, preferred_element_type=jnp.float32)
    aggregated = aggregate.reshape(feat_rows, node_cols).astype(jnp.bfloat16)
    w_slab = lax.dynamic_slice_in_dim(weight, col_pos * unit_rows, unit_rows, 1)
    pre_act = lax.dot_general(
        w_slab,
        lax.all_gather(aggregated, "cols", axis=0, tiled=True),
        (((0,), (0,)), ((), ())),
        preferred_element_type=jnp.float32,
    )
    output_t = jax.nn.silu(pre_act).astype(jnp.bfloat16)
    sigm = jax.nn.sigmoid(pre_act)
    pre_grad = (cotangent_t.astype(jnp.float32) * sigm * (1.0 + pre_act * (1.0 - sigm))).astype(
        jnp.bfloat16
    )
    w_mine = lax.dynamic_slice_in_dim(weight, col_pos * feat_rows, feat_rows, 0)
    portion = lax.all_gather(pre_grad, "cols", axis=0, tiled=True)
    grad_acc = jnp.dot(w_mine, portion, preferred_element_type=jnp.float32)
    block_grad = lax.dot_general(
        aggregated, portion, (((1,), (1,)), ((), ())), preferred_element_type=jnp.float32
    )
    grad_scale = 1.0 / math.sqrt(node_cols * row_devs)
    weight_grad = lax.psum(block_grad, "rows") * grad_scale
    agg_grad = grad_acc.astype(jnp.bfloat16)
    contrib = jnp.einsum(
        "fbi,bkij->bkfj",
        agg_grad.reshape(feat_rows, blocks_n, tile_n),
        adj_weight,
        preferred_element_type=jnp.float32,
    )
    contrib_flat = contrib.reshape(blocks_n * slots_n, feat_rows * tile_n)
    buffer = jax.ops.segment_sum(contrib_flat, own_flat, num_segments=row_devs * blocks_n)
    buffer = buffer.reshape(row_devs * blocks_n, feat_rows, tile_n)
    summed = lax.psum_scatter(buffer, "rows", scatter_dimension=0, tiled=True)
    feat_grad = summed.transpose(1, 0, 2).reshape(feat_rows, node_cols)
    return (output_t, weight_grad, feat_grad)


def solution(mesh):
    return jax.shard_map(
        body,
        mesh=mesh,
        in_specs=(P("cols", "rows"), P(), P("rows", None, None, None), P(), P("cols", "rows")),
        out_specs=(P("cols", "rows"), P("cols", None), P("cols", "rows")),
        check_vma=False,
    )
```

profile of v0, /device:TPU:4, one launch (start us, length us, event | category | flops | bytes accessed | tf_op | source)
XLA Modules:
  0.0 468.2 jit_solution(11323263088289372892)
XLA Ops:
  7.2 0.0 copy-start
  7.2 0.0 copy-start.3
  7.2 0.0 all-gather.3.cloned.1.call-start
  7.2 1.0 copy.36
  8.2 0.7 copy.22
  8.9 0.0 all-gather.3.cloned.1.call-update
  8.9 0.0 all-gather.5.cloned.1.call-start
  9.0 0.8 compare_select_fusion
  9.8 0.1 copy.23
  9.8 0.1 reshape.30
  9.9 87.4 %all-gather.3.cloned.1.call-done = bf16[1024,32,128]{2,1,0:T(8,128)(2,1)} async-done(((bf16[16,32,128]{2,1,0:T(8,128)(2,1)}), bf16[1024,32,128]{2,1,0:T(8,128)(2,1)}) %all-gather.3.cloned.1.call-update) | async-done | bytes 8388624 | tf_op jit(solution)/shard_map/all_gather | solution.py:20
  97.4 4.4 gather_fusion
  101.7 6.2 %fusion.5 = bf16[16,4,8,128]{3,2,1,0:T(8,128)(2,1)S(1)} fusion(bf16[16,16,32,128]{3,2,1,0:T(8,128)(2,1)S(1)} %bitcast.45, bf16[16,16,128,128]{3,2,1,0:T(8,128)(2,1)} %param.7), kind=kOutput, calls=%fused_computation.9 | convolution fusion | flops 268500992 | bytes 10616832 | tf_op jit(solution)/shard_map/bkfj,bkij->fbi/dot_general | solution.py:22
  108.0 11.6 %all_gather.10 = bf16[128,2048]{1,0:T(8,128)(2,1)S(1)} all-gather(bf16[32,2048]{1,0:T(8,128)(2,1)S(1)} %bitcast.47), channel_id=1, replica_groups=mesh['rows'=64,'cols'=4] {'cols'}, dimensions={0}, use_global_device_ids=true | all-gather | bytes 655360 | tf_op jit(solution)/shard_map/all_gather | solution.py:27
  119.5 0.0 copy-done
  119.5 0.0 copy-done.3
  119.5 1.3 multiply_convert_fusion
  120.8 0.0 all-gather.5.cloned.1.call-update
  120.9 0.2 reduce-scatter.2.cloned.1.call-start
  121.1 0.1 copy.25
  121.2 0.1 reshape.38
  121.3 24.2 %all-gather.5.cloned.1.call-done = bf16[256,2048]{1,0:T(8,128)(2,1)} async-done(((bf16[64,2048]{1,0:T(8,128)(2,1)}), bf16[256,2048]{1,0:T(8,128)(2,1)}) %all-gather.5.cloned.1.call-update) | async-done | bytes 1048592 | tf_op jit(solution)/shard_map/all_gather | solution.py:37
  145.5 1.5 fusion.6
  147.0 6.5 %fusion.7 = f32[16,32,16,128]{3,1,2,0:T(8,128)} fusion(bf16[16,16,128,128]{3,2,1,0:T(8,128)(2,1)} %param.7, bf16[32,16,128,1]{2,1,0,3:T(8,128)(2,1)S(1)} %bitcast.46), kind=kOutput, calls=%fused_computation.16 | convolution fusion | flops 268435456 | bytes 12713984 | tf_op jit(solution)/shard_map/fbi,bkij->bkfj/dot_general | solution.py:45
  153.6 16.7 %scatter_custom_fusion = f32[1024,4096]{1,0:T(8,128)} fusion(s32[256]{0:T(256)S(1)} %reshape.38, f32[]{:T(128)} %constant.11.clone.1, f32[32,8,32,128]{3,2,1,0:T(8,128)} %bitcast.44), kind=kCustom, calls=%fused_computation.2 | custom fusion | flops 1048576 | bytes 20971524 | tf_op jit(solution)/shard_map/scatter-add | solution.py:52
  170.3 17.5 %copy.27 = f32[1024,4096]{0,1:T(8,128)} copy(f32[1024,4096]{1,0:T(8,128)} %scatter_custom_fusion) | data formatting | bytes 33554432 | tf_op jit(solution)/shard_map/scatter-add | solution.py:52
  187.7 17.4 %copy.28 = f32[1024,32,128]{2,1,0:T(8,128)} copy(f32[1024,32,128]{0,2,1:T(8,128)} %bitcast.43) | data formatting | bytes 33554432 | tf_op jit(solution)/shard_map/reshape | solution.py:53
  205.1 0.0 copy-start.1
  205.1 0.0 copy-start.2
  205.1 0.0 reduce-scatter.2.cloned.1.call-update
  205.2 1.2 copy-done.2
  206.4 0.4 fusion.14
  206.8 252.5 %psum.7 = f32[32,256]{1,0:T(8,128)S(1)} all-reduce(f32[32,256]{1,0:T(8,128)S(1)} %fusion.14), channel_id=1, replica_groups=mesh['rows'=64,'cols'=4] {'rows'}, use_global_device_ids=true, to_apply=%region_0.1 | all-reduce | flops 8192 | bytes 65536 | tf_op jit(solution)/shard_map/psum | solution.py:43
  459.4 0.6 broadcast_multiply_fusion
  460.0 0.0 reduce-scatter.2.cloned.1.call-done
  460.0 1.7 copy_bitcast_fusion
  461.6 0.0 copy-done.1
  (3 shorter events, 0.1 us)
Async XLA Ops:
  7.2 112.4 %copy-start = (bf16[128,256]{1,0:T(8,128)(2,1)S(1)}, bf16[128,256]{1,0:T(8,128)(2,1)}, u32[]{:S(2)}) copy-start(bf16[128,256]{1,0:T(8,128)(2,1)} %param.8) | copy-start | bytes 196612
  7.2 112.4 %copy-start.3 = (bf16[64,2048]{1,0:T(8,128)(2,1)S(1)}, bf16[64,2048]{1,0:T(8,128)(2,1)}, u32[]{:S(2)}) copy-start(bf16[64,2048]{1,0:T(8,128)(2,1)} %param.9) | copy-start | bytes 786436
  7.2 90.2 %all-gather.3.cloned.1.call-start = ((), (), s32[]{:S(2)}) async-start(), calls=%async_computation.1 | async-start | bytes 8519680 | tf_op jit(solution)/shard_map/all_gather | solution.py:20
  8.9 136.6 %all-gather.5.cloned.1.call-start = ((), (), s32[]{:S(2)}) async-start(), calls=%async_computation.2 | async-start | bytes 1310720 | tf_op jit(solution)/shard_map/all_gather | solution.py:37
  120.9 339.1 %reduce-scatter.2.cloned.1.call-start = ((), (), s32[]{:S(2)}) async-start(), calls=%async_computation.3 | async-start | bytes 17039360 | tf_op jit(solution)/shard_map/reduce_scatter | solution.py:54
  205.1 256.5 %copy-start.1 = (bf16[128,256]{1,0:T(8,128)(2,1)S(1)}, bf16[128,256]{1,0:T(8,128)(2,1)}, u32[]{:S(2)}) copy-start(bf16[128,256]{1,0:T(8,128)(2,1)} %param.8) | copy-start | bytes 196612
  205.1 1.3 copy-start.2
Sparse Core Ops, SparseCore 0:
  11.4 85.9 all-gather.2
  121.0 24.4 all-gather.4
  205.3 191.1 reduce-scatter.1
where the time goes:
time: 469 us; the launch traced here: 468 us
  blocking collectives  264 us (56%)
  waiting for transfers between devices  112 us (24%)
  local copies, waits for them, and re-layouts  44.2 us (9%)
  other arithmetic  18.1 us (4%)
  matrix products  15.9 us (3%)
  between operations  13.8 us (3%)
    psum x1, blocking collectives, body(): weight_grad = lax.psum(block_grad, 'rows') * grad_scale  253 us
    all_gather x1, waiting for transfers between devices, body(): whole_panel = lax.all_gather(local_tiles, 'rows', axis=0, tiled=True)  87.4 us
    all_gather x1, waiting for transfers between devices, body(): portion = lax.all_gather(pre_grad, 'cols', axis=0, tiled=True)  24.2 us
    scatter-add x1, local copies, waits for them, and re-layouts, body(): jax.ops.segment_sum(contrib_flat, own_flat, num_segments=row_devs * block...  17.5 us
    reshape x1, local copies, waits for them, and re-layouts, body(): buffer = buffer.reshape(row_devs * blocks_n, feat_rows, tile_n)  17.4 us
    scatter-add x1, other arithmetic, body(): jax.ops.segment_sum(contrib_flat, own_flat, num_segments=row_devs * block...  16.7 us
    all_gather x1, blocking collectives, body(): lax.all_gather(aggregated, 'cols', axis=0, tiled=True)  11.6 us
  transfers between devices with their start and end apart: 3, of which 2 were waited for; matrix products, arithmetic and copies ran while one was open for 0% of the time, Pallas kernels for 0%

commit v1 on v0

--- a/solution.py
+++ b/solution.py
@@ -3,6 +3,22 @@
 import jax.numpy as jnp
 from jax import lax
 from jax.sharding import PartitionSpec as P
+
+
+def ring_gather(x, axis, dim):
+    ways, here, step = (lax.axis_size(axis), lax.axis_index(axis), x.shape[dim])
+    lengths = [n * ways if d == dim else n for d, n in enumerate(x.shape)]
+    full = lax.dynamic_update_slice_in_dim(jnp.zeros(lengths, x.dtype), x, here * step, axis=dim)
+    going_up = going_down = x
+    for far in range(1, ways // 2 + 1):
+        going_up = lax.ppermute(going_up, axis, [(d, (d + 1) % ways) for d in range(ways)])
+        full = lax.dynamic_update_slice_in_dim(full, going_up, (here - far) % ways * step, axis=dim)
+        if 2 * far < ways:
+            going_down = lax.ppermute(going_down, axis, [(d, (d - 1) % ways) for d in range(ways)])
+            full = lax.dynamic_update_slice_in_dim(
+                full, going_down, (here + far) % ways * step, axis=dim
+            )
+    return full
 
 
 def body(feats_t, adj_index, adj_weight, weight, cotangent_t):
@@ -34,7 +50,7 @@
         jnp.bfloat16
     )
     w_mine = lax.dynamic_slice_in_dim(weight, col_pos * feat_rows, feat_rows, 0)
-    portion = lax.all_gather(pre_grad, "cols", axis=0, tiled=True)
+    portion = ring_gather(pre_grad, "cols", 0)
     grad_acc = jnp.dot(w_mine, portion, preferred_element_type=jnp.float32)
     block_grad = lax.dot_general(
         aggregated, portion, (((1,), (1,)), ((), ())), preferred_element_type=jnp.float32

time: 469 us -> 454 us (0.968)
  waiting for transfers between devices: 112 us -> 96.8 us
  starting transfers between devices: 0.3 us -> 5.61 us
    all_gather x1 -> x0, waiting for transfers between devices: 24.2 us -> none  [body(): portion = lax.all_gather(pre_grad, 'cols', axis=0, tiled=True)]
    ppermute x0 -> x3, waiting for transfers between devices: none -> 9.31 us  [the longest x2 9.31 us: ring_gather(): lax.ppermute(going_up, axis, [(d, (d + 1) % ways) for d in range(ways)])]
    ppermute x0 -> x3, starting transfers between devices: none -> 5.53 us  [the longest x2 5.53 us: ring_gather(): lax.ppermute(going_up, axis, [(d, (d + 1) % ways) for d in range(ways)])]
  transfers between devices with their start and end apart: 3 -> 5, of which waited for: 2 -> 3; matrix products, arithmetic and copies ran while one was open for 0% -> 0% of each run, Pallas kernels for 0% -> 0%
where the time goes in v1:
time: 454 us; the launch traced here: 452 us
  blocking collectives  260 us (57%)
  waiting for transfers between devices  96.8 us (21%)
  local copies, waits for them, and re-layouts  43.1 us (9%)
  other arithmetic  18.3 us (4%)
  matrix products  14.6 us (3%)
  between operations  14.1 us (3%)
  starting transfers between devices  5.61 us (1%)
    psum x1, blocking collectives, body(): weight_grad = lax.psum(block_grad, 'rows') * grad_scale  248 us
    all_gather x1, waiting for transfers between devices, body(): whole_panel = lax.all_gather(local_tiles, 'rows', axis=0, tiled=True)  87.5 us
    scatter-add x1, local copies, waits for them, and re-layouts, body(): jax.ops.segment_sum(contrib_flat, own_flat, num_segments=row_devs * block...  17.5 us
    reshape x1, local copies, waits for them, and re-layouts, body(): buffer = buffer.reshape(row_devs * blocks_n, feat_rows, tile_n)  17.4 us
    scatter-add x1, other arithmetic, body(): jax.ops.segment_sum(contrib_flat, own_flat, num_segments=row_devs * block...  16.7 us
    all_gather x1, blocking collectives, body(): lax.all_gather(aggregated, 'cols', axis=0, tiled=True)  11.6 us
    ppermute x2, waiting for transfers between devices, ring_gather(): lax.ppermute(going_up, axis, [(d, (d + 1) % ways) for d in range(ways)])  9.31 us
  transfers between devices with their start and end apart: 5, of which 3 were waited for; matrix products, arithmetic and copies ran while one was open for 0% of the time, Pallas kernels for 0%

profile of v1, /device:TPU:4, one launch (start us, length us, event | category | flops | bytes accessed | tf_op | source)
XLA Modules:
  0.0 452.2 jit_solution(1975222242274011367)
XLA Ops:
  7.2 0.0 copy-start
  7.2 0.0 all-gather.2.cloned.1.call-start
  7.2 0.9 copy.36
  8.2 0.7 copy.22
  8.8 0.0 all-gather.2.cloned.1.call-update
  8.9 0.0 reduce-scatter.2.cloned.1.call-start
  8.9 0.8 compare_select_fusion
  9.7 0.1 copy.23
  9.8 0.1 reshape.30
  9.9 87.5 %all-gather.2.cloned.1.call-done = bf16[1024,32,128]{2,1,0:T(8,128)(2,1)} async-done(((bf16[16,32,128]{2,1,0:T(8,128)(2,1)}), bf16[1024,32,128]{2,1,0:T(8,128)(2,1)}) %all-gather.2.cloned.1.call-update) | async-done | bytes 8388624 | tf_op jit(solution)/shard_map/all_gather | solution.py:36
  97.4 4.4 gather_fusion
  101.7 0.0 copy-start.2
  101.8 6.2 %fusion.5 = bf16[16,4,8,128]{3,2,1,0:T(8,128)(2,1)S(1)} fusion(bf16[16,16,32,128]{3,2,1,0:T(8,128)(2,1)S(1)} %bitcast.45, bf16[16,16,128,128]{3,2,1,0:T(8,128)(2,1)} %param.7), kind=kOutput, calls=%fused_computation.9 | convolution fusion | flops 268500992 | bytes 10616832 | tf_op jit(solution)/shard_map/bkfj,bkij->fbi/dot_general | solution.py:38
  108.0 11.6 %all_gather.7 = bf16[128,2048]{1,0:T(8,128)(2,1)S(1)} all-gather(bf16[32,2048]{1,0:T(8,128)(2,1)S(1)} %bitcast.47), channel_id=1, replica_groups=mesh['rows'=64,'cols'=4] {'cols'}, dimensions={0}, use_global_device_ids=true | all-gather | bytes 655360 | tf_op jit(solution)/shard_map/all_gather | solution.py:43
  119.6 0.0 copy-done
  119.6 1.1 multiply_convert_fusion.1
  120.7 0.1 broadcast_in_dim.10
  120.8 0.0 copy-done.2
  120.8 0.2 constant_dynamic-update-slice_fusion.3
  121.0 3.0 collective-permute-start
  124.1 0.0 collective-permute-start.1
  124.1 0.1 copy.25
  124.1 0.1 reshape.38
  124.2 5.5 %collective-permute-done = bf16[64,2048]{1,0:T(8,128)(2,1)S(1)} collective-permute-done((bf16[64,2048]{1,0:T(8,128)(2,1)S(1)}, bf16[64,2048]{1,0:T(8,128)(2,1)S(1)}, u32[]{:S(2)}, u32[]{:S(2)}) %collective-permute-start) | collective-permute-done | bytes 262176 | tf_op jit(solution)/shard_map/ppermute | solution.py:14
  129.7 2.5 collective-permute-start.2
  132.2 0.0 collective-permute-done.1
  132.3 3.8 collective-permute-done.2
  136.1 0.3 fusion.6
  136.4 6.5 %fusion.7 = f32[16,32,16,128]{3,1,2,0:T(8,128)} fusion(bf16[16,16,128,128]{3,2,1,0:T(8,128)(2,1)} %param.7, bf16[32,16,128,1]{2,1,0,3:T(8,128)(2,1)S(1)} %bitcast.46), kind=kOutput, calls=%fused_computation.16 | convolution fusion | flops 268435456 | bytes 12713984 | tf_op jit(solution)/shard_map/fbi,bkij->bkfj/dot_general | solution.py:61
  143.0 16.7 %scatter_custom_fusion = f32[1024,4096]{1,0:T(8,128)} fusion(s32[256]{0:T(256)S(1)} %reshape.38, f32[]{:T(128)} %constant.59.clone.1, f32[32,8,32,128]{3,2,1,0:T(8,128)} %bitcast.44), kind=kCustom, calls=%fused_computation.2 | custom fusion | flops 1048576 | bytes 20971524 | tf_op jit(solution)/shard_map/scatter-add | solution.py:68
  159.7 17.5 %copy.27 = f32[1024,4096]{0,1:T(8,128)} copy(f32[1024,4096]{1,0:T(8,128)} %scatter_custom_fusion) | data formatting | bytes 33554432 | tf_op jit(solution)/shard_map/scatter-add | solution.py:68
  177.1 17.4 %copy.28 = f32[1024,32,128]{2,1,0:T(8,128)} copy(f32[1024,32,128]{0,2,1:T(8,128)} %bitcast.43) | data formatting | bytes 33554432 | tf_op jit(solution)/shard_map/reshape | solution.py:69
  194.5 0.0 copy-start.1
  194.5 0.0 reduce-scatter.2.cloned.1.call-update
  194.6 0.4 fusion.14
  195.0 248.1 %psum.7 = f32[32,256]{1,0:T(8,128)S(1)} all-reduce(f32[32,256]{1,0:T(8,128)S(1)} %fusion.14), channel_id=1, replica_groups=mesh['rows'=64,'cols'=4] {'rows'}, use_global_device_ids=true, to_apply=%region_0.1 | all-reduce | flops 8192 | bytes 65536 | tf_op jit(solution)/shard_map/psum | solution.py:59
  443.1 0.6 broadcast_multiply_fusion
  443.7 0.0 reduce-scatter.2.cloned.1.call-done
  443.7 1.7 copy_bitcast_fusion
  445.3 0.0 copy-done.1
  (6 shorter events, 0.1 us)
Async XLA Ops:
  7.2 112.4 %copy-start = (bf16[128,256]{1,0:T(8,128)(2,1)S(1)}, bf16[128,256]{1,0:T(8,128)(2,1)}, u32[]{:S(2)}) copy-start(bf16[128,256]{1,0:T(8,128)(2,1)} %param.8) | copy-start | bytes 196612
  7.2 90.2 %all-gather.2.cloned.1.call-start = ((), (), s32[]{:S(2)}) async-start(), calls=%async_computation.1 | async-start | bytes 8519680 | tf_op jit(solution)/shard_map/all_gather | solution.py:36
  8.9 434.8 %reduce-scatter.2.cloned.1.call-start = ((), (), s32[]{:S(2)}) async-start(), calls=%async_computation.2 | async-start | bytes 17039360 | tf_op jit(solution)/shard_map/reduce_scatter | solution.py:70
  101.7 19.1 %copy-start.2 = (bf16[64,2048]{1,0:T(8,128)(2,1)S(1)}, bf16[64,2048]{1,0:T(8,128)(2,1)}, u32[]{:S(2)}) copy-start(bf16[64,2048]{1,0:T(8,128)(2,1)} %param.9) | copy-start | bytes 786436
  121.0 8.7 %collective-permute-start = (bf16[64,2048]{1,0:T(8,128)(2,1)S(1)}, bf16[64,2048]{1,0:T(8,128)(2,1)S(1)}, u32[]{:S(2)}, u32[]{:S(2)}) collective-permute-start(bf16[64,2048]{1,0:T(8,128)(2,1)S(1)} %get-tuple-element.4), channel_id=1, source_target_pairs={{0,1},{1,2},{2,3},{3,0},{4,5},{5,6},{6,7},{7,4},{8,9},{9,10},{10,1... | collective-permute-start | bytes 786440 | tf_op jit(solution)/shard_map/ppermute | solution.py:14
  124.1 8.2 %collective-permute-start.1 = (bf16[64,2048]{1,0:T(8,128)(2,1)S(1)}, bf16[64,2048]{1,0:T(8,128)(2,1)S(1)}, u32[]{:S(2)}, u32[]{:S(2)}) collective-permute-start(bf16[64,2048]{1,0:T(8,128)(2,1)S(1)} %get-tuple-element.4), channel_id=1, source_target_pairs={{0,3},{1,0},{2,1},{3,2},{4,7},{5,4},{6,5},{7,6},{8,11},{9,8},{10,9... | collective-permute-start | bytes 786440 | tf_op jit(solution)/shard_map/ppermute | solution.py:17
  129.7 6.4 %collective-permute-start.2 = (bf16[64,2048]{1,0:T(8,128)(2,1)S(1)}, bf16[64,2048]{1,0:T(8,128)(2,1)S(1)}, u32[]{:S(2)}, u32[]{:S(2)}) collective-permute-start(bf16[64,2048]{1,0:T(8,128)(2,1)S(1)} %collective-permute-done), channel_id=1, source_target_pairs={{0,1},{1,2},{2,3},{3,0},{4,5},{5,6},{6,7},{7,4},{8,9},{9,10},{10,1... | collective-permute-start | bytes 786440 | tf_op jit(solution)/shard_map/ppermute | solution.py:14
  194.5 250.8 %copy-start.1 = (bf16[128,256]{1,0:T(8,128)(2,1)S(1)}, bf16[128,256]{1,0:T(8,128)(2,1)}, u32[]{:S(2)}) copy-start(bf16[128,256]{1,0:T(8,128)(2,1)} %param.8) | copy-start | bytes 196612
Sparse Core Ops, SparseCore 0:
  11.4 85.9 all-gather.1
  194.7 188.3 reduce-scatter.1
